TPU v7x, 256 devices: a whole 4x4x8 slice. The times are simulated.
256 devices in a mesh: shot: 128 (over x, y, z), freq: 2 (over core).
Axes of the slice: x: 4, y: 4, z: 8, core: 2. Of those that a mesh axis runs over, the one named last changes fastest.
Arguments:
- traces: bfloat16 [256, 1024, 1024], P('shot', None, 'freq'), may hold values from -6 to 6
- frequency_bins: int32 [8], replicated, may hold values from 1 to 511
- aperture: int32 [256, 1024, 32], P(None, 'shot'), may hold values from 0 to 255, as said below
- lengths: int32 [256, 1024], P(None, 'shot'), may hold values from 1 to 32, as said below
- filters: bfloat16 [256, 31], P('shot'), may hold values from -1 to 1
Outputs:
- multiples: bfloat16 [256, 1024, 1024], P('shot', None, 'freq')
Inputs may be any that keep to these rules, and one draw needn't show every extreme that they name: aperture[s, r, k] names a shot whose source lies at receiver station 4 times that number; only entries with k below lengths[s, r] are used. The lengths of the shots held by one device along `shot` (one index of the `shot` axis) and the receivers of one index of shot sum to at most 264; in every draw the shots of some index reach 264 with the receivers of every index.
All inputs are finite; a program needn't handle non-finite values.
Results may differ from a plain program's by a relative error of at most 0.015.
Values may be sent and summed in bfloat16 or wider, within the bound.
A program may use at most 192 MiB of HBM per device.

v0:
```python
import math
import jax
import jax.numpy as jnp
from jax import lax
from jax.sharding import PartitionSpec as P

NT = 1024
NF = 8
KMAX = 32
TAPS = 31


def extended(shard, sides, width):
    for axis, dim in sides:
        devices, length = (lax.axis_size(axis), shard.shape[dim])
        up = [(i, (i + 1) % devices) for i in range(devices - 1)]
        down = [(j, i) for i, j in up]
        last = lax.slice_in_dim(shard, length - width, length, axis=dim)
        leading = lax.slice_in_dim(shard, 0, width, axis=dim)
        before = lax.ppermute(last, axis, up)
        after = lax.ppermute(leading, axis, down)
        shard = jnp.concatenate([before, shard, after], axis=dim)
    return shard


def fourier_rows(bin_rows, first_time, sample_count, period):
    sample_times = first_time + jnp.arange(sample_count, dtype=jnp.int32)
    phases = bin_rows[:, None] * sample_times[None, :] % period
    angles = phases.astype(jnp.float32) * (2.0 * math.pi / period)
    return (jnp.cos(angles), jnp.sin(angles))


def pair_product(first_leg, second):
    first_leg = first_leg.astype(jnp.float32)
    second = second.astype(jnp.float32)
    real_part = first_leg[:, 0] * second[:, 0] - first_leg[:, 1] * second[:, 1]
    imag_part = first_leg[:, 0] * second[:, 1] + first_leg[:, 1] * second[:, 0]
    return jnp.stack([real_part, imag_part], axis=1)


def pick_columns(table, codes):
    block_width = 2048
    column_count = table.shape[1]
    wanted = codes.shape[0]
    block_count = -(-wanted // block_width)
    extra = block_count * block_width - wanted
    codes = jnp.concatenate([codes.astype(jnp.int32), jnp.full((extra,), -1, jnp.int32)]).reshape(
        block_count, block_width
    )
    column_ids = jnp.arange(column_count, dtype=jnp.int32)[:, None]

    def one_block(block_codes):
        onehot = (column_ids == block_codes[None, :]).astype(jnp.bfloat16)
        return jnp.dot(table, onehot, preferred_element_type=jnp.float32).astype(jnp.bfloat16)

    picked = lax.map(one_block, codes)
    picked = picked.transpose(1, 0, 2).reshape(table.shape[0], block_count * block_width)
    return picked


def pick_each(tables, codes):

    def one_table(inputs):
        return pick_columns(inputs[0], inputs[1])

    return lax.map(one_table, (tables, codes))


def shards(traces, frequency_bins, aperture, lengths, filters):
    shot_dev, receivers, time_dev = traces.shape
    groups = lax.axis_size("shot")
    shots = shot_dev * groups
    receiver_dev = receivers // groups
    stride = receivers // shots
    local_bins = NF // lax.axis_size("freq")
    start_time = lax.axis_index("freq") * time_dev
    half_taps = (TAPS - 1) // 2
    flat_traces = traces.reshape(shot_dev * receivers, time_dev)
    bin_rows = frequency_bins
    cosines, sines = fourier_rows(bin_rows, start_time, time_dev, NT)
    basis_rows = (jnp.stack([cosines, -sines], axis=1) * NT ** (-0.5)).astype(jnp.bfloat16)
    basis_rows = basis_rows.reshape(lax.axis_size("freq") * local_bins * 2, time_dev)
    term = lax.dot_general(
        basis_rows, flat_traces, (((1,), (1,)), ((), ())), preferred_element_type=jnp.float32
    )
    spectra = lax.psum_scatter(
        term.reshape(lax.axis_size("freq") * local_bins, 2, shot_dev, receivers),
        "freq",
        scatter_dimension=0,
        tiled=True,
    ).astype(jnp.bfloat16)
    gathers = lax.all_to_all(spectra, "shot", split_axis=3, concat_axis=2, tiled=True)
    valid_mask = jnp.arange(KMAX, dtype=jnp.int32)[None, None, :] < lengths[:, :, None]
    station_rows = spectra[:, :, :, ::stride].reshape(local_bins * 2, shot_dev * shots)
    receiver_tables = gathers.reshape(local_bins * 2, shots, receiver_dev).transpose(2, 0, 1)
    list_width = receiver_dev * KMAX
    used_codes = (
        jnp.where(valid_mask, aperture, -1).transpose(1, 0, 2).reshape(receiver_dev, shots * KMAX)
    )
    second = pick_each(receiver_tables, used_codes).reshape(
        receiver_dev, local_bins * 2, shots, KMAX
    )
    second = second.transpose(1, 2, 0, 3).reshape(local_bins * 2, groups, shot_dev, list_width)
    labels = aperture.reshape(1, groups, shot_dev, list_width)
    second, labels = (
        lax.all_to_all(second, "shot", split_axis=1, concat_axis=1, tiled=True),
        lax.all_to_all(labels, "shot", split_axis=1, concat_axis=1, tiled=True),
    )
    station_tables = station_rows.reshape(local_bins * 2, shot_dev, shots).transpose(1, 0, 2)
    station_codes = labels[0].transpose(1, 0, 2).reshape(shot_dev, groups * list_width)
    first_leg = pick_each(station_tables, station_codes).reshape(
        shot_dev, local_bins * 2, groups, list_width
    )
    first_leg = first_leg.transpose(1, 2, 0, 3)
    block_shape = (local_bins, 2, groups, shot_dev, list_width)
    product_terms = pair_product(first_leg.reshape(block_shape), second.reshape(block_shape))
    product_terms = product_terms.reshape(local_bins, 2, groups, shot_dev, receiver_dev, KMAX).sum(
        axis=-1
    )
    summed = product_terms.transpose(0, 1, 3, 2, 4).reshape(local_bins, 2, shot_dev, receivers)
    multiples_spectra = (summed * KMAX ** (-0.5)).astype(jnp.bfloat16)
    piece = lax.all_gather(multiples_spectra, "freq", axis=0, tiled=True)
    row_count = piece.shape[0]
    bin_rows = frequency_bins
    cosines, sines = fourier_rows(bin_rows, start_time, time_dev, NT)
    basis_rows = (
        jnp.stack([cosines, -sines], axis=1).astype(jnp.bfloat16).reshape(row_count * 2, time_dev)
    )
    flat_piece = piece.reshape(row_count * 2, shot_dev * receivers)
    synthesized = lax.dot_general(
        flat_piece, basis_rows, (((0,), (0,)), ((), ())), preferred_element_type=jnp.float32
    )
    predicted = synthesized.astype(jnp.bfloat16).reshape(shot_dev, receivers, time_dev)
    padded = extended(predicted, (("freq", 2),), half_taps)
    padded_width = time_dev + 2 * half_taps
    lag_table = (
        jnp.arange(time_dev, dtype=jnp.int32)[None, :]
        + 2 * half_taps
        - jnp.arange(padded_width, dtype=jnp.int32)[:, None]
    )
    tap_onehot = (lag_table[None] == jnp.arange(TAPS, dtype=jnp.int32)[:, None, None]).astype(
        jnp.bfloat16
    )
    toeplitz = jnp.einsum(
        "sj,jut->sut", filters, tap_onehot, preferred_element_type=jnp.float32
    ).astype(jnp.bfloat16)
    filtered = jnp.einsum("sru,sut->srt", padded, toeplitz, preferred_element_type=jnp.float32)
    return filtered.astype(jnp.bfloat16)


def solution(mesh):
    in_specs = (
        P("shot", None, "freq"),
        P(),
        P(None, "shot", None),
        P(None, "shot"),
        P("shot", None),
    )
    out_specs = P("shot", None, "freq")
    return jax.shard_map(shards, mesh=mesh, in_specs=in_specs, out_specs=out_specs, check_vma=False)
```

profile of v0, /device:TPU:1, one launch (start us, length us, event | category | flops | bytes accessed | tf_op | source)
XLA Modules:
  0.0 197.0 jit_solution(6553147078118205570)
XLA Ops:
  2.2 7.1 %all-reduce.2 = bf16[8,2,2,1024]{3,0,2,1:T(8,128)(2,1)S(1)} all-reduce(f32[8,2,2,1024]{3,0,2,1:T(8,128)S(1)} %fusion.18), channel_id=2, replica_groups=mesh['shot'=128,'freq'=2] {'freq'}, use_global_device_ids=true, to_apply=%region_0.1.clone | all-reduce | flops 32768 | bytes 196608
  10.6 2.1 %copy.49 = bf16[4,2,2,1024]{0,2,1,3:T(2,128)(2,1)} copy(bf16[4,2,2,1024]{3,0,2,1:T(4,128)(2,1)S(1)} %dynamic-slice_convert_fusion) | data formatting | bytes 65536 | tf_op jit(solution)/shard_map/convert_element_type | solution.py:91
  12.7 14.3 %all-to-all-start.1 = ((bf16[4,2,2,1024]{0,2,1,3:T(2,128)(2,1)}), bf16[4,2,2,1024]{0,2,1,3:T(2,128)(2,1)}, u32[]{:S(2)}, u32[]{:S(2)}) async-start(bf16[4,2,2,1024]{0,2,1,3:T(2,128)(2,1)} %copy.49), calls=%async_computation.1 | async-start | bytes 2097152 | tf_op jit(solution)/shard_map/all_to_all | solution.py:92
  28.7 2.3 %copy.48 = s32[8,256,32]{2,1,0:T(8,128)} copy(s32[8,256,32]{1,2,0:T(8,128)} %select_bitcast_fusion) | data formatting | bytes 524288 | tf_op jit(solution)/shard_map/transpose | solution.py:98
  31.0 2.4 %reshape.222 = s32[8,8192]{1,0:T(8,128)} reshape(s32[8,256,32]{2,1,0:T(8,128)} %copy.48) | data formatting | bytes 524288 | tf_op jit(solution)/shard_map/reshape | solution.py:98
  36.5 21.0 %all-to-all-done.1 = bf16[4,2,2,1024]{0,2,1,3:T(2,128)(2,1)} async-done(((bf16[4,2,2,1024]{0,2,1,3:T(2,128)(2,1)}), bf16[4,2,2,1024]{0,2,1,3:T(2,128)(2,1)}, u32[]{:S(2)}, u32[]{:S(2)}) %all-to-all-start.1) | async-done | bytes 32800 | tf_op jit(solution)/shard_map/all_to_all | solution.py:92
  57.5 6.4 %all-to-all-start = ((s32[1,128,2,256]{3,2,0,1:T(2,128)}), s32[1,128,2,256]{3,2,0,1:T(2,128)S(1)}, u32[]{:S(2)}, u32[]{:S(2)}) async-start(s32[1,128,2,256]{3,2,0,1:T(2,128)} %bitcast.6), calls=%async_computation | async-start | bytes 524288 | tf_op jit(solution)/shard_map/all_to_all | solution.py:107
  63.9 5.0 %copy.65 = bf16[4,2,2,128,8]{4,3,2,1,0:T(8,128)(2,1)S(1)} copy(bf16[4,2,2,128,8]{0,2,1,4,3:T(2,128)(2,1)} %bitcast.18) | data formatting | bytes 65536 | tf_op jit(solution)/shard_map/all_to_all | solution.py:92
  69.6 28.5 %while.45 = (s32[]{:T(128)}, bf16[8,8,8192]{2,1,0:T(8,128)(2,1)}, s32[8,8192]{1,0:T(8,128)}, bf16[8,8,256]{2,1,0:T(8,128)(2,1)S(1)}, s32[]{:T(128)}, /*index=5*/s32[]{:T(128)}, s32[]{:T(128)}) while((s32[]{:T(128)}, bf16[8,8,8192]{2,1,0:T(8,128)(2,1)}, s32[8,8192]{1,0:T(8,128)}, bf16[8,8,256]{2,1,0:T(8,128)(2,1)S(1)}, s32[]{:T(128)}, ...), condition=%wide.region_8.9_spmd, body=%wide.region_5.8_spmd.sunk | while | flops 8929284 | bytes 463562 | solution.py:66
  98.1 5.6 %reshape.224 = bf16[8,8,256,32]{3,2,1,0:T(8,128)(2,1)} reshape(bf16[8,8,8192]{2,1,0:T(8,128)(2,1)} %get-tuple-element.104) | data formatting | bytes 2097152 | tf_op jit(solution)/shard_map/reshape | solution.py:100
  103.7 6.8 %copy.53 = bf16[8,256,8,32]{3,2,0,1:T(8,128)(2,1)} copy(bf16[8,256,8,32]{3,1,0,2:T(8,128)(2,1)} %bitcast.104) | data formatting | bytes 2097152 | tf_op jit(solution)/shard_map/transpose | solution.py:103
  110.6 6.2 %reshape.225 = bf16[8,128,2,256]{3,0,2,1:T(8,128)(2,1)} reshape(bf16[8,256,8,32]{3,2,0,1:T(8,128)(2,1)} %copy.53) | data formatting | bytes 2097152 | tf_op jit(solution)/shard_map/reshape | solution.py:103
  116.7 13.6 %all-to-all-start.2 = ((bf16[8,128,2,256]{3,0,2,1:T(8,128)(2,1)}), bf16[8,128,2,256]{3,0,2,1:T(8,128)(2,1)}, u32[]{:S(2)}, u32[]{:S(2)}) async-start(bf16[8,128,2,256]{3,0,2,1:T(8,128)(2,1)} %reshape.225), calls=%async_computation.2 | async-start | bytes 2097152 | tf_op jit(solution)/shard_map/all_to_all | solution.py:106
  130.4 16.9 %while.43 = (s32[]{:T(128)}, bf16[2,8,32768]{2,1,0:T(8,128)(2,1)}, s32[2,32768]{1,0:T(2,128)S(1)}, bf16[2,8,256]{2,1,0:T(8,128)(2,1)S(1)}, s32[]{:T(128)}, /*index=5*/s32[]{:T(128)}, s32[]{:T(128)}) while((s32[]{:T(128)}, bf16[2,8,32768]{2,1,0:T(8,128)(2,1)}, s32[2,32768]{1,0:T(2,128)S(1)}, bf16[2,8,256]{2,1,0:T(8,128)(2,1)S(1)}, s32[]{:T(128)}, ...), condition=%wide.region_4.5_spmd, body=%wide.region_1.4_spmd.sunk | while | flops 8929284 | bytes 1643210 | solution.py:66
  130.8 7.2 %while.46 = (s32[]{:T(128)}, bf16[16,8,2048]{2,1,0:T(8,128)(2,1)S(1)}, s32[16,2048]{1,0:T(8,128)S(1)}, bf16[8,256]{1,0:T(8,128)(2,1)S(1)}, s32[]{:T(128)}) while((s32[]{:T(128)}, bf16[16,8,2048]{2,1,0:T(8,128)(2,1)S(1)}, s32[16,2048]{1,0:T(8,128)S(1)}, bf16[8,256]{1,0:T(8,128)(2,1)S(1)}, s32[]{:T(128)}) %tuple.81), condition=%wide.region_3.3_spmd.clone, body=%wide.region_2.2_spmd.clone.sunk | while | flops 8929282 | bytes 61509 | solution.py:56
  139.2 7.2 %while.46 = (s32[]{:T(128)}, bf16[16,8,2048]{2,1,0:T(8,128)(2,1)S(1)}, s32[16,2048]{1,0:T(8,128)S(1)}, bf16[8,256]{1,0:T(8,128)(2,1)S(1)}, s32[]{:T(128)}) while((s32[]{:T(128)}, bf16[16,8,2048]{2,1,0:T(8,128)(2,1)S(1)}, s32[16,2048]{1,0:T(8,128)S(1)}, bf16[8,256]{1,0:T(8,128)(2,1)S(1)}, s32[]{:T(128)}) %tuple.81), condition=%wide.region_3.3_spmd.clone, body=%wide.region_2.2_spmd.clone.sunk | while | flops 8929282 | bytes 61509 | solution.py:56
  150.2 8.3 %all-to-all-done.2 = bf16[8,128,2,256]{3,0,2,1:T(8,128)(2,1)} async-done(((bf16[8,128,2,256]{3,0,2,1:T(8,128)(2,1)}), bf16[8,128,2,256]{3,0,2,1:T(8,128)(2,1)}, u32[]{:S(2)}, u32[]{:S(2)}) %all-to-all-start.2) | async-done | bytes 1048608 | tf_op jit(solution)/shard_map/all_to_all | solution.py:106
  163.6 2.5 %copy.56 = f32[4,1,128,2,256]{2,4,3,0,1:T(8,128)} copy(f32[4,1,128,2,256]{4,2,3,1,0:T(8,128)} %get-tuple-element.182) | data formatting | bytes 2097152 | tf_op jit(solution)/shard_map/add | solution.py:37
  168.5 6.0 %all_gather.3 = bf16[8,2,2,1024]{3,2,1,0:T(2,128)(2,1)S(1)} all-gather(bf16[4,2,2,1024]{3,2,1,0:T(2,128)(2,1)S(1)} %convert_element_type.101), channel_id=1, replica_groups=mesh['shot'=128,'freq'=2] {'freq'}, dimensions={0}, use_global_device_ids=true | all-gather | bytes 98304 | tf_op jit(solution)/shard_map/all_gather | solution.py:122
  174.6 2.1 %convolution_convert_fusion.2 = bf16[2048,512]{1,0:T(8,128)(2,1)} fusion(bf16[16,2048]{1,0:T(8,128)(2,1)S(1)} %bitcast.118, bf16[16,512]{1,0:T(8,128)(2,1)S(1)} %copy-done.5), kind=kOutput, calls=%fused_computation.23 | convolution fusion | flops 34603008 | bytes 2179072 | tf_op jit(solution)/shard_map/dot_general | solution.py:130
  176.6 4.1 %copy.59 = bf16[2,1024,512]{1,2,0:T(8,128)(2,1)} copy(bf16[2,1024,512]{2,1,0:T(8,128)(2,1)} %bitcast.108) | data formatting | bytes 4194304 | tf_op jit(solution)/shard_map/reshape | solution.py:133
  182.9 3.2 %collective-permute-start.1 = (bf16[2,1024,15]{1,2,0:T(8,128)(2,1)S(1)}, bf16[2,1024,15]{1,2,0:T(8,128)(2,1)S(1)}, u32[]{:S(2)}, u32[]{:S(2)}) collective-permute-start(bf16[2,1024,15]{1,2,0:T(8,128)(2,1)S(1)} %get-tuple-element.184), channel_id=1, source_target_pairs={{1,0},{3,2},{5,4},{7,6},{9,8},{11,10},{13,12},{15,14},{17,16},{19,... | collective-permute-start | bytes 184328 | tf_op jit(solution)/shard_map/ppermute | solution.py:21
  186.1 7.7 %fusion.24 = bf16[2,542,512]{2,0,1:T(2,128)(2,1)S(1)} fusion(s32[542,512]{1,0:T(8,128)S(1)} %copy-done.3, bf16[2,31]{1,0:T(2,128)(2,1)S(1)} %copy-done.7), kind=kOutput, calls=%fused_computation.36 | convolution fusion | flops 43568128 | bytes 2220156 | tf_op jit(solution)/shard_map/sj,jut->sut/dot_general | solution.py:144
  193.8 3.2 %fusion.20 = bf16[2,1024,512]{2,1,0:T(8,128)(2,1)} fusion(bf16[2,1024,15]{1,2,0:T(8,128)(2,1)S(1)} %collective-permute-done.1, bf16[2,1024,512]{1,2,0:T(8,128)(2,1)S(1)} %copy-done.2, bf16[2,1024,15]{1,2,0:T(8,128)(2,1)S(1)} %collective-permute-done, bf16[2,542,512]{2,0,1:T(2,128)(2,1)S(1)} %fusion.24), kind=kOutput, calls=%fused_computation.34 | convolution fusion | flops 1144365056 | bytes 5427200 | tf_op jit(solution)/shard_map/sru,sut->srt/dot_general | solution.py:147
  (239 shorter events, 79.9 us)
Async XLA Ops:
  0.0 1.6 copy-start
  0.0 9.3 %copy-start.8 = (u32[256]{0:T(256)S(1)}, u32[256]{0:T(256)}, u32[]{:S(2)}) copy-start(u32[256]{0:T(256)} %constant.92) | copy-start | bytes 3076
  2.2 25.3 %copy-start.4 = (s32[256,8,32]{0,2,1:T(8,128)S(1)}, s32[256,8,32]{0,2,1:T(8,128)}, u32[]{:S(2)}) copy-start(s32[256,8,32]{0,2,1:T(8,128)} %param.15) | copy-start | bytes 786436
  10.6 17.4 %copy-start.6 = (s32[256,8]{0,1:T(8,128)S(1)}, s32[256,8]{0,1:T(8,128)}, u32[]{:S(2)}) copy-start(s32[256,8]{0,1:T(8,128)} %param.16) | copy-start | bytes 24580
  12.7 44.8 %all-to-all-start.1 = ((bf16[4,2,2,1024]{0,2,1,3:T(2,128)(2,1)}), bf16[4,2,2,1024]{0,2,1,3:T(2,128)(2,1)}, u32[]{:S(2)}, u32[]{:S(2)}) async-start(bf16[4,2,2,1024]{0,2,1,3:T(2,128)(2,1)} %copy.49), calls=%async_computation.1 | async-start | bytes 2097152 | tf_op jit(solution)/shard_map/all_to_all | solution.py:92
  57.5 59.2 %all-to-all-start = ((s32[1,128,2,256]{3,2,0,1:T(2,128)}), s32[1,128,2,256]{3,2,0,1:T(2,128)S(1)}, u32[]{:S(2)}, u32[]{:S(2)}) async-start(s32[1,128,2,256]{3,2,0,1:T(2,128)} %bitcast.6), calls=%async_computation | async-start | bytes 524288 | tf_op jit(solution)/shard_map/all_to_all | solution.py:107
  116.7 41.8 %all-to-all-start.2 = ((bf16[8,128,2,256]{3,0,2,1:T(8,128)(2,1)}), bf16[8,128,2,256]{3,0,2,1:T(8,128)(2,1)}, u32[]{:S(2)}, u32[]{:S(2)}) async-start(bf16[8,128,2,256]{3,0,2,1:T(8,128)(2,1)} %reshape.225), calls=%async_computation.2 | async-start | bytes 2097152 | tf_op jit(solution)/shard_map/all_to_all | solution.py:106
  158.5 1.9 copy-start.1
  166.1 8.5 %copy-start.5 = (bf16[16,512]{1,0:T(8,128)(2,1)S(1)}, bf16[16,512]{1,0:T(8,128)(2,1)}, u32[]{:S(2)}) copy-start(bf16[16,512]{1,0:T(8,128)(2,1)} %convert_element_type.103) | copy-start | bytes 49156
  176.6 9.4 %copy-start.3 = (s32[542,512]{1,0:T(8,128)S(1)}, s32[542,512]{1,0:T(8,128)}, u32[]{:S(2)}) copy-start(s32[542,512]{1,0:T(8,128)} %iota_subtract_fusion) | copy-start | bytes 3330052
  176.6 9.4 %copy-start.7 = (bf16[2,31]{1,0:T(2,128)(2,1)S(1)}, bf16[2,31]{1,0:T(2,128)(2,1)}, u32[]{:S(2)}) copy-start(bf16[2,31]{1,0:T(2,128)(2,1)} %param.17) | copy-start | bytes 376
  181.6 12.2 %collective-permute-start = (bf16[2,1024,15]{1,2,0:T(8,128)(2,1)S(1)}, bf16[2,1024,15]{1,2,0:T(8,128)(2,1)S(1)}, u32[]{:S(2)}, u32[]{:S(2)}) collective-permute-start(bf16[2,1024,15]{1,2,0:T(8,128)(2,1)S(1)} %get-tuple-element.183), channel_id=1, source_target_pairs={{0,1},{2,3},{4,5},{6,7},{8,9},{10,11},{12,13},{14,15},{16,17},{18,... | collective-permute-start | bytes 184328 | tf_op jit(solution)/shard_map/ppermute | solution.py:20
  182.9 10.9 %copy-start.2 = (bf16[2,1024,512]{1,2,0:T(8,128)(2,1)S(1)}, bf16[2,1024,512]{1,2,0:T(8,128)(2,1)}, u32[]{:S(2)}) copy-start(bf16[2,1024,512]{1,2,0:T(8,128)(2,1)} %copy.59) | copy-start | bytes 6291460
  182.9 10.9 %collective-permute-start.1 = (bf16[2,1024,15]{1,2,0:T(8,128)(2,1)S(1)}, bf16[2,1024,15]{1,2,0:T(8,128)(2,1)S(1)}, u32[]{:S(2)}, u32[]{:S(2)}) collective-permute-start(bf16[2,1024,15]{1,2,0:T(8,128)(2,1)S(1)} %get-tuple-element.184), channel_id=1, source_target_pairs={{1,0},{3,2},{5,4},{7,6},{9,8},{11,10},{13,12},{15,14},{17,16},{19,... | collective-permute-start | bytes 184328 | tf_op jit(solution)/shard_map/ppermute | solution.py:21
where the time goes:
time: 198 us; the launch traced here: 197 us
  local copies, waits for them, and re-layouts  66.8 us (34%)
  matrix products  41 us (21%)
  starting transfers between devices  38.7 us (20%)
  waiting for transfers between devices  29.3 us (15%)
  blocking collectives  13.1 us (7%)
  other arithmetic  6.15 us (3%)
    dot_general x64, matrix products, one_block(): jnp.dot(table, onehot, preferred_element_type=jnp.float32)  27.5 us
    all_to_all x1, waiting for transfers between devices, shards(): lax.all_to_all(spectra, 'shot', split_axis=3, concat_axis=2, tiled=True)  21 us
    all_to_all x1, starting transfers between devices, shards(): lax.all_to_all(spectra, 'shot', split_axis=3, concat_axis=2, tiled=True)  14.3 us
    all_to_all x1, starting transfers between devices, shards(): lax.all_to_all(second, 'shot', split_axis=1, concat_axis=1, tiled=True)  13.6 us
    dynamic_slice x10, local copies, waits for them, and re-layouts, pick_each(): return lax.map(one_table, (tables, codes))  9.08 us
    all_to_all x1, waiting for transfers between devices, shards(): lax.all_to_all(second, 'shot', split_axis=1, concat_axis=1, tiled=True)  8.31 us
    dot_general x1, matrix products, shards(): jnp.einsum('sj,jut->sut', filters, tap_onehot, preferred_element_type=jnp...  7.66 us
    unnamed x1, blocking collectives  7.06 us
  transfers between devices with their start and end apart: 5, of which 2 were waited for; matrix products, arithmetic and copies ran while one was open for 45% of the time, Pallas kernels for 0%

commit v1 on v0

--- a/solution.py
+++ b/solution.py
@@ -119,7 +119,9 @@
     )
     summed = product_terms.transpose(0, 1, 3, 2, 4).reshape(local_bins, 2, shot_dev, receivers)
     multiples_spectra = (summed * KMAX ** (-0.5)).astype(jnp.bfloat16)
-    piece = lax.all_gather(multiples_spectra, "freq", axis=0, tiled=True)
+    piece = jnp.concatenate(
+        lax.all_to_all(jnp.stack([multiples_spectra] * lax.axis_size("freq")), "freq", 0, 0), axis=0
+    )
     row_count = piece.shape[0]
     bin_rows = frequency_bins
     cosines, sines = fourier_rows(bin_rows, start_time, time_dev, NT)

time: 198 us -> 200 us (1.010)
    all_to_all x0 -> x1, blocking collectives: none -> 7.82 us  [shards(): lax.all_to_all(jnp.stack([multiples_spectra] * lax.axis_size('freq')), 'f...]
    all_gather x1 -> x0, blocking collectives: 6.04 us -> none  [shards(): piece = lax.all_gather(multiples_spectra, 'freq', axis=0, tiled=True)]
where the time goes in v1:
time: 200 us; the launch traced here: 199 us
  local copies, waits for them, and re-layouts  66.8 us (33%)
  matrix products  41 us (20%)
  starting transfers between devices  38.7 us (19%)
  waiting for transfers between devices  29.3 us (15%)
  blocking collectives  14.9 us (7%)
  other arithmetic  6.2 us (3%)
    dot_general x64, matrix products, one_block(): jnp.dot(table, onehot, preferred_element_type=jnp.float32)  27.5 us
    all_to_all x1, waiting for transfers between devices, shards(): lax.all_to_all(spectra, 'shot', split_axis=3, concat_axis=2, tiled=True)  21 us
    all_to_all x1, starting transfers between devices, shards(): lax.all_to_all(spectra, 'shot', split_axis=3, concat_axis=2, tiled=True)  14.3 us
    all_to_all x1, starting transfers between devices, shards(): lax.all_to_all(second, 'shot', split_axis=1, concat_axis=1, tiled=True)  13.6 us
    dynamic_slice x10, local copies, waits for them, and re-layouts, pick_each(): return lax.map(one_table, (tables, codes))  9.08 us
    all_to_all x1, waiting for transfers between devices, shards(): lax.all_to_all(second, 'shot', split_axis=1, concat_axis=1, tiled=True)  8.31 us
    all_to_all x1, blocking collectives, shards(): lax.all_to_all(jnp.stack([multiples_spectra] * lax.axis_size('freq')), 'f...  7.82 us
    dot_general x1, matrix products, shards(): jnp.einsum('sj,jut->sut', filters, tap_onehot, preferred_element_type=jnp...  7.66 us
  transfers between devices with their start and end apart: 5, of which 2 were waited for; matrix products, arithmetic and copies ran while one was open for 45% of the time, Pallas kernels for 0%

profile of v1, /device:TPU:1, one launch (start us, length us, event | category | flops | bytes accessed | tf_op | source)
XLA Modules:
  0.0 198.8 jit_solution(11954286997857112756)
XLA Ops:
  2.2 7.1 %all-reduce.2 = bf16[8,2,2,1024]{3,0,2,1:T(8,128)(2,1)S(1)} all-reduce(f32[8,2,2,1024]{3,0,2,1:T(8,128)S(1)} %fusion.18), channel_id=2, replica_groups=mesh['shot'=128,'freq'=2] {'freq'}, use_global_device_ids=true, to_apply=%region_0.1.clone | all-reduce | flops 32768 | bytes 196608
  10.6 2.1 %copy.49 = bf16[4,2,2,1024]{0,2,1,3:T(2,128)(2,1)} copy(bf16[4,2,2,1024]{3,0,2,1:T(4,128)(2,1)S(1)} %dynamic-slice_convert_fusion) | data formatting | bytes 65536 | tf_op jit(solution)/shard_map/convert_element_type | solution.py:91
  12.7 14.3 %all-to-all-start.1 = ((bf16[4,2,2,1024]{0,2,1,3:T(2,128)(2,1)}), bf16[4,2,2,1024]{0,2,1,3:T(2,128)(2,1)}, u32[]{:S(2)}, u32[]{:S(2)}) async-start(bf16[4,2,2,1024]{0,2,1,3:T(2,128)(2,1)} %copy.49), calls=%async_computation.1 | async-start | bytes 2097152 | tf_op jit(solution)/shard_map/all_to_all | solution.py:92
  28.7 2.3 %copy.48 = s32[8,256,32]{2,1,0:T(8,128)} copy(s32[8,256,32]{1,2,0:T(8,128)} %select_bitcast_fusion) | data formatting | bytes 524288 | tf_op jit(solution)/shard_map/transpose | solution.py:98
  31.0 2.4 %reshape.232 = s32[8,8192]{1,0:T(8,128)} reshape(s32[8,256,32]{2,1,0:T(8,128)} %copy.48) | data formatting | bytes 524288 | tf_op jit(solution)/shard_map/reshape | solution.py:98
  36.5 21.0 %all-to-all-done.1 = bf16[4,2,2,1024]{0,2,1,3:T(2,128)(2,1)} async-done(((bf16[4,2,2,1024]{0,2,1,3:T(2,128)(2,1)}), bf16[4,2,2,1024]{0,2,1,3:T(2,128)(2,1)}, u32[]{:S(2)}, u32[]{:S(2)}) %all-to-all-start.1) | async-done | bytes 32800 | tf_op jit(solution)/shard_map/all_to_all | solution.py:92
  57.5 6.4 %all-to-all-start = ((s32[1,128,2,256]{3,2,0,1:T(2,128)}), s32[1,128,2,256]{3,2,0,1:T(2,128)S(1)}, u32[]{:S(2)}, u32[]{:S(2)}) async-start(s32[1,128,2,256]{3,2,0,1:T(2,128)} %bitcast.6), calls=%async_computation | async-start | bytes 524288 | tf_op jit(solution)/shard_map/all_to_all | solution.py:107
  63.9 5.0 %copy.65 = bf16[4,2,2,128,8]{4,3,2,1,0:T(8,128)(2,1)S(1)} copy(bf16[4,2,2,128,8]{0,2,1,4,3:T(2,128)(2,1)} %bitcast.18) | data formatting | bytes 65536 | tf_op jit(solution)/shard_map/all_to_all | solution.py:92
  69.6 28.5 %while.45 = (s32[]{:T(128)}, bf16[8,8,8192]{2,1,0:T(8,128)(2,1)}, s32[8,8192]{1,0:T(8,128)}, bf16[8,8,256]{2,1,0:T(8,128)(2,1)S(1)}, s32[]{:T(128)}, /*index=5*/s32[]{:T(128)}, s32[]{:T(128)}) while((s32[]{:T(128)}, bf16[8,8,8192]{2,1,0:T(8,128)(2,1)}, s32[8,8192]{1,0:T(8,128)}, bf16[8,8,256]{2,1,0:T(8,128)(2,1)S(1)}, s32[]{:T(128)}, ...), condition=%wide.region_8.9_spmd, body=%wide.region_5.8_spmd.sunk | while | flops 8929284 | bytes 463562 | solution.py:66
  98.1 5.6 %reshape.234 = bf16[8,8,256,32]{3,2,1,0:T(8,128)(2,1)} reshape(bf16[8,8,8192]{2,1,0:T(8,128)(2,1)} %get-tuple-element.104) | data formatting | bytes 2097152 | tf_op jit(solution)/shard_map/reshape | solution.py:100
  103.7 6.8 %copy.53 = bf16[8,256,8,32]{3,2,0,1:T(8,128)(2,1)} copy(bf16[8,256,8,32]{3,1,0,2:T(8,128)(2,1)} %bitcast.104) | data formatting | bytes 2097152 | tf_op jit(solution)/shard_map/transpose | solution.py:103
  110.6 6.2 %reshape.235 = bf16[8,128,2,256]{3,0,2,1:T(8,128)(2,1)} reshape(bf16[8,256,8,32]{3,2,0,1:T(8,128)(2,1)} %copy.53) | data formatting | bytes 2097152 | tf_op jit(solution)/shard_map/reshape | solution.py:103
  116.7 13.6 %all-to-all-start.2 = ((bf16[8,128,2,256]{3,0,2,1:T(8,128)(2,1)}), bf16[8,128,2,256]{3,0,2,1:T(8,128)(2,1)}, u32[]{:S(2)}, u32[]{:S(2)}) async-start(bf16[8,128,2,256]{3,0,2,1:T(8,128)(2,1)} %reshape.235), calls=%async_computation.2 | async-start | bytes 2097152 | tf_op jit(solution)/shard_map/all_to_all | solution.py:106
  130.4 16.9 %while.43 = (s32[]{:T(128)}, bf16[2,8,32768]{2,1,0:T(8,128)(2,1)}, s32[2,32768]{1,0:T(2,128)S(1)}, bf16[2,8,256]{2,1,0:T(8,128)(2,1)S(1)}, s32[]{:T(128)}, /*index=5*/s32[]{:T(128)}, s32[]{:T(128)}) while((s32[]{:T(128)}, bf16[2,8,32768]{2,1,0:T(8,128)(2,1)}, s32[2,32768]{1,0:T(2,128)S(1)}, bf16[2,8,256]{2,1,0:T(8,128)(2,1)S(1)}, s32[]{:T(128)}, ...), condition=%wide.region_4.5_spmd, body=%wide.region_1.4_spmd.sunk | while | flops 8929284 | bytes 1643210 | solution.py:66
  130.8 7.2 %while.46 = (s32[]{:T(128)}, bf16[16,8,2048]{2,1,0:T(8,128)(2,1)S(1)}, s32[16,2048]{1,0:T(8,128)S(1)}, bf16[8,256]{1,0:T(8,128)(2,1)S(1)}, s32[]{:T(128)}) while((s32[]{:T(128)}, bf16[16,8,2048]{2,1,0:T(8,128)(2,1)S(1)}, s32[16,2048]{1,0:T(8,128)S(1)}, bf16[8,256]{1,0:T(8,128)(2,1)S(1)}, s32[]{:T(128)}) %tuple.81), condition=%wide.region_3.3_spmd.clone, body=%wide.region_2.2_spmd.clone.sunk | while | flops 8929282 | bytes 61509 | solution.py:56
  139.2 7.2 %while.46 = (s32[]{:T(128)}, bf16[16,8,2048]{2,1,0:T(8,128)(2,1)S(1)}, s32[16,2048]{1,0:T(8,128)S(1)}, bf16[8,256]{1,0:T(8,128)(2,1)S(1)}, s32[]{:T(128)}) while((s32[]{:T(128)}, bf16[16,8,2048]{2,1,0:T(8,128)(2,1)S(1)}, s32[16,2048]{1,0:T(8,128)S(1)}, bf16[8,256]{1,0:T(8,128)(2,1)S(1)}, s32[]{:T(128)}) %tuple.81), condition=%wide.region_3.3_spmd.clone, body=%wide.region_2.2_spmd.clone.sunk | while | flops 8929282 | bytes 61509 | solution.py:56
  150.2 8.3 %all-to-all-done.2 = bf16[8,128,2,256]{3,0,2,1:T(8,128)(2,1)} async-done(((bf16[8,128,2,256]{3,0,2,1:T(8,128)(2,1)}), bf16[8,128,2,256]{3,0,2,1:T(8,128)(2,1)}, u32[]{:S(2)}, u32[]{:S(2)}) %all-to-all-start.2) | async-done | bytes 1048608 | tf_op jit(solution)/shard_map/all_to_all | solution.py:106
  163.6 2.5 %copy.56 = f32[4,1,128,2,256]{2,4,3,0,1:T(8,128)} copy(f32[4,1,128,2,256]{4,2,3,1,0:T(8,128)} %get-tuple-element.182) | data formatting | bytes 2097152 | tf_op jit(solution)/shard_map/add | solution.py:37
  168.6 7.8 %all_to_all.30 = bf16[2,4,2,2,1024]{4,3,2,1,0:T(2,128)(2,1)S(1)} all-to-all(bf16[2,4,2,2,1024]{4,3,2,1,0:T(2,128)(2,1)S(1)} %pad_maximum_fusion), channel_id=1, replica_groups=mesh['shot'=128,'freq'=2] {'freq'}, dimensions={0} | all-to-all | bytes 131072 | tf_op jit(solution)/shard_map/all_to_all | solution.py:123
  176.4 2.1 %convolution_convert_fusion.2 = bf16[2048,512]{1,0:T(8,128)(2,1)} fusion(bf16[16,2048]{1,0:T(8,128)(2,1)S(1)} %bitcast.118, bf16[16,512]{1,0:T(8,128)(2,1)S(1)} %copy-done.5), kind=kOutput, calls=%fused_computation.23 | convolution fusion | flops 34603008 | bytes 2179072 | tf_op jit(solution)/shard_map/dot_general | solution.py:132
  178.5 4.1 %copy.59 = bf16[2,1024,512]{1,2,0:T(8,128)(2,1)} copy(bf16[2,1024,512]{2,1,0:T(8,128)(2,1)} %bitcast.108) | data formatting | bytes 4194304 | tf_op jit(solution)/shard_map/reshape | solution.py:135
  184.7 3.2 %collective-permute-start.1 = (bf16[2,1024,15]{1,2,0:T(8,128)(2,1)S(1)}, bf16[2,1024,15]{1,2,0:T(8,128)(2,1)S(1)}, u32[]{:S(2)}, u32[]{:S(2)}) collective-permute-start(bf16[2,1024,15]{1,2,0:T(8,128)(2,1)S(1)} %get-tuple-element.184), channel_id=1, source_target_pairs={{1,0},{3,2},{5,4},{7,6},{9,8},{11,10},{13,12},{15,14},{17,16},{19,... | collective-permute-start | bytes 184328 | tf_op jit(solution)/shard_map/ppermute | solution.py:21
  187.9 7.7 %fusion.24 = bf16[2,542,512]{2,0,1:T(2,128)(2,1)S(1)} fusion(s32[542,512]{1,0:T(8,128)S(1)} %copy-done.3, bf16[2,31]{1,0:T(2,128)(2,1)S(1)} %copy-done.7), kind=kOutput, calls=%fused_computation.36 | convolution fusion | flops 43568128 | bytes 2220156 | tf_op jit(solution)/shard_map/sj,jut->sut/dot_general | solution.py:146
  195.6 3.2 %fusion.20 = bf16[2,1024,512]{2,1,0:T(8,128)(2,1)} fusion(bf16[2,1024,15]{1,2,0:T(8,128)(2,1)S(1)} %collective-permute-done.1, bf16[2,1024,512]{1,2,0:T(8,128)(2,1)S(1)} %copy-done.2, bf16[2,1024,15]{1,2,0:T(8,128)(2,1)S(1)} %collective-permute-done, bf16[2,542,512]{2,0,1:T(2,128)(2,1)S(1)} %fusion.24), kind=kOutput, calls=%fused_computation.34 | convolution fusion | flops 1144365056 | bytes 5427200 | tf_op jit(solution)/shard_map/sru,sut->srt/dot_general | solution.py:149
  (240 shorter events, 79.9 us)
Async XLA Ops:
  0.0 1.6 copy-start
  0.0 9.3 %copy-start.8 = (u32[256]{0:T(256)S(1)}, u32[256]{0:T(256)}, u32[]{:S(2)}) copy-start(u32[256]{0:T(256)} %constant.92) | copy-start | bytes 3076
  2.2 25.3 %copy-start.4 = (s32[256,8,32]{0,2,1:T(8,128)S(1)}, s32[256,8,32]{0,2,1:T(8,128)}, u32[]{:S(2)}) copy-start(s32[256,8,32]{0,2,1:T(8,128)} %param.15) | copy-start | bytes 786436
  10.6 17.4 %copy-start.6 = (s32[256,8]{0,1:T(8,128)S(1)}, s32[256,8]{0,1:T(8,128)}, u32[]{:S(2)}) copy-start(s32[256,8]{0,1:T(8,128)} %param.16) | copy-start | bytes 24580
  12.7 44.8 %all-to-all-start.1 = ((bf16[4,2,2,1024]{0,2,1,3:T(2,128)(2,1)}), bf16[4,2,2,1024]{0,2,1,3:T(2,128)(2,1)}, u32[]{:S(2)}, u32[]{:S(2)}) async-start(bf16[4,2,2,1024]{0,2,1,3:T(2,128)(2,1)} %copy.49), calls=%async_computation.1 | async-start | bytes 2097152 | tf_op jit(solution)/shard_map/all_to_all | solution.py:92
  57.5 59.2 %all-to-all-start = ((s32[1,128,2,256]{3,2,0,1:T(2,128)}), s32[1,128,2,256]{3,2,0,1:T(2,128)S(1)}, u32[]{:S(2)}, u32[]{:S(2)}) async-start(s32[1,128,2,256]{3,2,0,1:T(2,128)} %bitcast.6), calls=%async_computation | async-start | bytes 524288 | tf_op jit(solution)/shard_map/all_to_all | solution.py:107
  116.7 41.8 %all-to-all-start.2 = ((bf16[8,128,2,256]{3,0,2,1:T(8,128)(2,1)}), bf16[8,128,2,256]{3,0,2,1:T(8,128)(2,1)}, u32[]{:S(2)}, u32[]{:S(2)}) async-start(bf16[8,128,2,256]{3,0,2,1:T(8,128)(2,1)} %reshape.235), calls=%async_computation.2 | async-start | bytes 2097152 | tf_op jit(solution)/shard_map/all_to_all | solution.py:106
  158.5 1.9 copy-start.1
  166.1 10.3 %copy-start.5 = (bf16[16,512]{1,0:T(8,128)(2,1)S(1)}, bf16[16,512]{1,0:T(8,128)(2,1)}, u32[]{:S(2)}) copy-start(bf16[16,512]{1,0:T(8,128)(2,1)} %convert_element_type.110) | copy-start | bytes 49156
  178.5 9.4 %copy-start.3 = (s32[542,512]{1,0:T(8,128)S(1)}, s32[542,512]{1,0:T(8,128)}, u32[]{:S(2)}) copy-start(s32[542,512]{1,0:T(8,128)} %iota_subtract_fusion) | copy-start | bytes 3330052
  178.5 9.4 %copy-start.7 = (bf16[2,31]{1,0:T(2,128)(2,1)S(1)}, bf16[2,31]{1,0:T(2,128)(2,1)}, u32[]{:S(2)}) copy-start(bf16[2,31]{1,0:T(2,128)(2,1)} %param.17) | copy-start | bytes 376
  183.4 12.2 %collective-permute-start = (bf16[2,1024,15]{1,2,0:T(8,128)(2,1)S(1)}, bf16[2,1024,15]{1,2,0:T(8,128)(2,1)S(1)}, u32[]{:S(2)}, u32[]{:S(2)}) collective-permute-start(bf16[2,1024,15]{1,2,0:T(8,128)(2,1)S(1)} %get-tuple-element.183), channel_id=1, source_target_pairs={{0,1},{2,3},{4,5},{6,7},{8,9},{10,11},{12,13},{14,15},{16,17},{18,... | collective-permute-start | bytes 184328 | tf_op jit(solution)/shard_map/ppermute | solution.py:20
  184.7 10.9 %copy-start.2 = (bf16[2,1024,512]{1,2,0:T(8,128)(2,1)S(1)}, bf16[2,1024,512]{1,2,0:T(8,128)(2,1)}, u32[]{:S(2)}) copy-start(bf16[2,1024,512]{1,2,0:T(8,128)(2,1)} %copy.59) | copy-start | bytes 6291460
  184.7 10.9 %collective-permute-start.1 = (bf16[2,1024,15]{1,2,0:T(8,128)(2,1)S(1)}, bf16[2,1024,15]{1,2,0:T(8,128)(2,1)S(1)}, u32[]{:S(2)}, u32[]{:S(2)}) collective-permute-start(bf16[2,1024,15]{1,2,0:T(8,128)(2,1)S(1)} %get-tuple-element.184), channel_id=1, source_target_pairs={{1,0},{3,2},{5,4},{7,6},{9,8},{11,10},{13,12},{15,14},{17,16},{19,... | collective-permute-start | bytes 184328 | tf_op jit(solution)/shard_map/ppermute | solution.py:21
